TPU v7x, 256 devices: a whole 4x4x8 slice. The times are simulated.
256 devices in a mesh: chan: 32 (over x, y, core), wide: 8 (over z).
Axes of the slice: x: 4, y: 4, z: 8, core: 2. Of those that a mesh axis runs over, the one named last changes fastest.
Arguments:
- conc_now: float32 [8, 64, 64, 1024], P(None, 'chan', None, 'wide'), may hold values from 0.01 to 1
- conc_prev: float32 [8, 64, 64, 1024], P(None, 'chan', None, 'wide'), may hold values from 0.1 to 1
- phi_prev: float32 [64, 64, 1024], P('chan', None, 'wide'), may hold values from -3 to 3
- owner: int32 [64, 64, 1024], P('chan', None, 'wide'), may hold values from 0 to 2048, as said below
- partner: int32 [2048], replicated, may hold values from 0 to 2047, each once
- valence: int32 [8], replicated, may hold values from -2 to 2
- diffusivity: float32 [8], replicated, may hold values from 0.2 to 1
Outputs:
- conc_next: float32 [8, 64, 64, 1024], P(None, 'chan', None, 'wide')
- potential: float32 [64, 64, 1024], P('chan', None, 'wide')
Inputs may be any that keep to these rules, and one draw needn't show every extreme that they name: `owner`: the value 2048 marks a cell of no junction. The cells of one junction lie within one block of 2 cells along the length and 128 along the width, aligned with the grid. Some junctions own no cell. `partner`: every junction appears once.
All inputs are finite; a program needn't handle non-finite values.
Results may differ from a plain program's by a relative error of at most 0.00029.
Values sent between devices are 32-bit elements; how exact they have to be, the bound alone decides.
A program may use at most 128 MiB of HBM per device.

v0:
```python
import math
import jax
import jax.numpy as jnp
from jax import lax
from jax.sharding import PartitionSpec as P

SWEEPS = 4
time_step = 0.5
coupling = 2.0
charge_scale = 0.05
conduct_ref = 1.5
highest = lax.Precision.HIGHEST


def with_halo(cells, sides, width):
    for axis, dim in sides:
        count = lax.axis_size(axis)
        ends = count - 1
        head = lax.slice_in_dim(cells, 0, width, axis=dim)
        tail = lax.slice_in_dim(cells, cells.shape[dim] - width, cells.shape[dim], axis=dim)
        cells = jnp.concatenate(
            [
                lax.ppermute(tail, axis, [(i, (i + 1) % count) for i in range(ends)]),
                cells,
                lax.ppermute(head, axis, [((i + 1) % count, i) for i in range(ends)]),
            ],
            axis=dim,
        )
    return cells


def sine_table(length):
    index = jnp.arange(length).astype(jnp.float32) + 1.0
    return math.sqrt(2.0 / (length + 1.0)) * jnp.sin(
        math.pi * index[:, None] * index[None, :] / (length + 1.0)
    )


def eigen_values(length):
    index = jnp.arange(length).astype(jnp.float32) + 1.0
    return 2.0 - 2.0 * jnp.cos(math.pi * index / (length + 1.0))


def conductivity(concs, valence, diffusivity):
    charge_sq = (valence * valence).astype(jnp.float32)
    weights = charge_sq * diffusivity / jnp.sum((charge_sq + 1.0) * diffusivity)
    return 1.0 + jnp.sum(weights[:, None, None, None] * concs * concs, axis=0)


def neighbours(padded, depth_mode):
    middle = padded[..., 1:-1, :, 1:-1]
    widths = [(0, 0)] * (padded.ndim - 3) + [(0, 0), (1, 1), (0, 0)]
    depth_padded = jnp.pad(middle, widths, mode=depth_mode)
    return [
        padded[..., :-2, :, 1:-1],
        padded[..., 2:, :, 1:-1],
        depth_padded[..., :-2, :],
        depth_padded[..., 2:, :],
        padded[..., 1:-1, :, :-2],
        padded[..., 1:-1, :, 2:],
    ]


def rim_replace(padded, lower_x, upper_x, lower_y, upper_y):
    low_plane = jnp.where(lower_x, padded[..., 1:2, :, :], padded[..., 0:1, :, :])
    high_plane = jnp.where(upper_x, padded[..., -2:-1, :, :], padded[..., -1:, :, :])
    padded = jnp.concatenate([low_plane, padded[..., 1:-1, :, :], high_plane], axis=-3)
    low_plane = jnp.where(lower_y, padded[..., 1:2], padded[..., 0:1])
    high_plane = jnp.where(upper_y, padded[..., -2:-1], padded[..., -1:])
    return jnp.concatenate([low_plane, padded[..., 1:-1], high_plane], axis=-1)


def halo_potential(potential_field):
    return with_halo(potential_field, (("chan", 0), ("wide", 2)), 1)


def per_device(conc_now, conc_prev, phi_prev, owner, partner, valence, diffusivity):
    species_all, cells_x, depth_all, cells_y = conc_now.shape
    chan_total = lax.axis_size("chan")
    wide_total = lax.axis_size("wide")
    chan_place = lax.axis_index("chan")
    wide_place = lax.axis_index("wide")
    length_all = cells_x * chan_total
    width_all = cells_y * wide_total
    depth_piece = depth_all // wide_total
    width_piece = width_all // chan_total
    junction_total = partner.shape[0]
    lower_x = chan_place == 0
    upper_x = chan_place == chan_total - 1
    lower_y = wide_place == 0
    upper_y = wide_place == wide_total - 1
    table_x = sine_table(length_all)
    table_z = sine_table(depth_all)
    table_y = sine_table(width_all)
    eigen_x = eigen_values(length_all)
    eigen_y = eigen_values(width_all)
    eigen_z = lax.dynamic_slice_in_dim(
        eigen_values(depth_all), wide_place * depth_piece, depth_piece
    )
    charge_weights = valence.astype(jnp.float32)[:, None, None, None]
    drift = (valence.astype(jnp.float32) * diffusivity)[:, None, None, None]
    spread = diffusivity[:, None, None, None]
    owners = jnp.minimum(owner.reshape(-1), junction_total)
    cell_counts = jax.ops.segment_sum(
        jnp.ones(owners.shape, jnp.float32), owners, num_segments=junction_total + 1
    )
    concs = conc_now
    potential_field = phi_prev
    conc_raw = with_halo(concs, (("chan", 1), ("wide", 3)), 1)
    sigma_local = conductivity(concs, valence, diffusivity)
    sigma_padded = with_halo(sigma_local, (("chan", 0), ("wide", 2)), 1)
    charge = charge_scale * jnp.sum(charge_weights * concs, axis=0)
    for sweep_step in range(SWEEPS):
        phi_padded = halo_potential(potential_field)
        apply_phi_near_all = neighbours(phi_padded, "constant")
        sigma_near_all = neighbours(sigma_padded, "constant")
        sigma_mid = sigma_padded[1:-1, :, 1:-1]
        applied = jnp.zeros_like(potential_field)
        for apply_phi_near, sigma_near in zip(apply_phi_near_all, sigma_near_all):
            applied = applied + 0.5 * (sigma_mid + sigma_near) * (potential_field - apply_phi_near)
        spectrum = jnp.einsum("az,xzy->xay", table_z, charge - applied, precision=highest)
        spectrum = lax.all_to_all(spectrum, "wide", split_axis=1, concat_axis=2, tiled=True)
        across = jnp.einsum("xzy,yb->xzb", spectrum, table_y, precision=highest)
        lined = lax.all_to_all(across, "chan", split_axis=2, concat_axis=0, tiled=True)
        lined = jnp.einsum("ax,xzy->azy", table_x, lined, precision=highest)
        eigen_part = lax.dynamic_slice_in_dim(eigen_y, chan_place * width_piece, width_piece)
        lined = lined / (
            conduct_ref
            * (eigen_x[:, None, None] + eigen_z[None, :, None] + eigen_part[None, None, :])
        )
        lined = jnp.einsum("ax,xzy->azy", table_x, lined, precision=highest)
        across = lax.all_to_all(lined, "chan", split_axis=0, concat_axis=2, tiled=True)
        spectrum = jnp.einsum("xzy,yb->xzb", across, table_y, precision=highest)
        spectrum = lax.all_to_all(spectrum, "wide", split_axis=2, concat_axis=1, tiled=True)
        potential_field = potential_field + jnp.einsum(
            "az,xzy->xay", table_z, spectrum, precision=highest
        )
    cell_rows = concs.reshape(species_all, -1).T
    junction_sums = jax.ops.segment_sum(cell_rows, owners, num_segments=junction_total + 1)
    junction_sums, total_counts = lax.psum((junction_sums, cell_counts), ("chan", "wide"))
    means = junction_sums / jnp.maximum(total_counts, 1.0)[:, None]
    own_means = means[:junction_total]
    table = coupling * (own_means[partner] - own_means)
    table = jnp.concatenate([table, jnp.zeros((1, species_all), jnp.float32)], axis=0)
    source = table[owners].T.reshape(concs.shape)
    conc_fixed = rim_replace(conc_raw, lower_x, upper_x, lower_y, upper_y)
    phi_fixed = rim_replace(halo_potential(potential_field), lower_x, upper_x, lower_y, upper_y)
    conc_near_all = neighbours(conc_fixed, "edge")
    phi_near_all = neighbours(phi_fixed, "edge")
    diagonal_part = jnp.zeros_like(concs) + 1.5 / time_step
    gathered_terms = (4.0 * conc_now - conc_prev) / (2.0 * time_step) + source
    for conc_near, phi_near in zip(conc_near_all, phi_near_all):
        velocity = drift * (potential_field - phi_near)[None]
        diagonal_part = diagonal_part + spread + jnp.maximum(velocity, 0.0)
        gathered_terms = gathered_terms + (spread + jnp.maximum(-velocity, 0.0)) * conc_near
    concs = gathered_terms / diagonal_part
    return (concs, potential_field)


def solution(mesh):
    return jax.shard_map(
        per_device,
        mesh=mesh,
        in_specs=(
            P(None, "chan", None, "wide"),
            P(None, "chan", None, "wide"),
            P("chan", None, "wide"),
            P("chan", None, "wide"),
            P(),
            P(),
            P(),
        ),
        out_specs=(P(None, "chan", None, "wide"), P("chan", None, "wide")),
        check_vma=False,
    )
```

profile of v0, /device:TPU:34, one launch (start us, length us, event | category | flops | bytes accessed | tf_op | source)
XLA Modules:
  0.0 887.7 jit_solution(6742743469902880809)
XLA Ops:
  29.9 5.4 collective-permute-done
  51.3 11.0 %all-to-all-start = ((f32[2,64,128]{2,0,1:T(2,128)}), f32[2,64,128]{2,0,1:T(2,128)S(1)}, u32[]{:S(2)}, u32[]{:S(2)}) async-start(f32[2,64,128]{2,0,1:T(2,128)} %copy.85), calls=%async_computation | async-start | bytes 131072 | tf_op jit(solution)/shard_map/all_to_all | solution.py:122
  62.4 6.8 all-to-all-done
  69.2 16.9 %fusion.14 = f32[2,8,1024]{2,1,0:T(8,128)S(1)} fusion(f32[1024]{0:T(1024)S(1)} %get-tuple-element.64, f32[1024]{0:T(1024)S(1)} %get-tuple-element.65, f32[2,8,8,128]{3,0,2,1:T(2,128)S(1)} %bitcast.241), kind=kOutput, calls=%fused_computation.18 | convolution fusion | flops 204472320 | bytes 139264 | tf_op jit(solution)/shard_map/xzy,yb->xzb/dot_general | solution.py:123
  93.9 6.2 all-to-all-done.1
  105.0 10.9 %all_to_all.288 = f32[32,1,512]{2,1,0:T(1,128)S(1)} all-to-all(f32[32,1,512]{2,1,0:T(1,128)S(1)} %reshape.173), channel_id=1, replica_groups=mesh['chan'=32,'wide'=8] {'chan'}, dimensions={0} | all-to-all | bytes 131072 | tf_op jit(solution)/shard_map/all_to_all | solution.py:132
  117.0 16.6 %fusion.12 = f32[2,8,1024]{2,1,0:T(8,128)S(1)} fusion(f32[2,8,1024]{2,1,0:T(8,128)S(1)} %all_to_all.219, f32[1024]{0:T(1024)S(1)} %get-tuple-element.64, f32[1024]{0:T(1024)S(1)} %get-tuple-element.65), kind=kOutput, calls=%fused_computation.16 | convolution fusion | flops 204472320 | bytes 139264 | tf_op jit(solution)/shard_map/xzy,yb->xzb/dot_general | solution.py:133
  135.8 10.8 %all_to_all.289 = f32[8,1,2048]{2,1,0:T(1,128)S(1)} all-to-all(f32[8,1,2048]{2,1,0:T(1,128)S(1)} %reshape.175), channel_id=1, replica_groups=mesh['chan'=32,'wide'=8] {'wide'}, dimensions={0} | all-to-all | bytes 131072 | tf_op jit(solution)/shard_map/all_to_all | solution.py:134
  154.2 5.4 collective-permute-done.8
  170.4 12.4 %all_to_all.290 = f32[2,64,128]{2,0,1:T(2,128)S(1)} all-to-all(f32[2,64,128]{2,0,1:T(2,128)S(1)} %copy.94), channel_id=1, replica_groups=mesh['chan'=32,'wide'=8] {'wide'}, dimensions={1} | all-to-all | bytes 131072 | tf_op jit(solution)/shard_map/all_to_all | solution.py:122
  182.8 16.6 %fusion.10 = f32[2,8,1024]{2,1,0:T(8,128)S(1)} fusion(f32[1024]{0:T(1024)S(1)} %get-tuple-element.64, f32[1024]{0:T(1024)S(1)} %get-tuple-element.65, f32[2,8,8,128]{3,0,2,1:T(2,128)S(1)} %bitcast.244), kind=kOutput, calls=%fused_computation.14 | convolution fusion | flops 204472320 | bytes 139264 | tf_op jit(solution)/shard_map/xzy,yb->xzb/dot_general | solution.py:123
  228.2 110.4 %scatter_custom_fusion = f32[2049,8]{1,0:T(8,128)} fusion(s32[16384]{0:T(1024)S(1)} %bitcast.237, f32[16384,8]{1,0:T(8,128)} %bitcast.196, f32[]{:T(128)} %constant.28.clone.1), kind=kCustom, calls=%fused_computation.84 | custom fusion | flops 131072 | bytes 66080 | tf_op jit(solution)/shard_map/scatter-add | solution.py:139
  339.7 16.8 %fusion.8 = f32[2,8,1024]{2,1,0:T(8,128)S(1)} fusion(f32[2,8,1024]{2,1,0:T(8,128)S(1)} %all_to_all.235, f32[1024]{0:T(1024)S(1)} %copy-done.21, f32[1024]{0:T(1024)S(1)} %copy-done.25), kind=kOutput, calls=%fused_computation.12 | convolution fusion | flops 204472320 | bytes 139264 | tf_op jit(solution)/shard_map/xzy,yb->xzb/dot_general | solution.py:133
  363.3 7.0 all-to-all-done.7
  378.4 109.7 %scatter_custom_fusion.1 = f32[2049]{0:T(1024)S(1)} fusion(s32[16384]{0:T(1024)S(1)} %bitcast.239, f32[16384]{0:T(1024)S(1)} %broadcast.172, f32[]{:T(128)} %constant.28.clone.1), kind=kCustom, calls=%fused_computation.420 | custom fusion | flops 16384 | bytes 8200 | tf_op jit(solution)/shard_map/scatter-add | solution.py:104
  494.1 79.7 %psum.15 = f32[2049]{0:T(1024)S(1)} all-reduce(f32[2049]{0:T(1024)S(1)} %scatter_custom_fusion.1), channel_id=1, replica_groups=mesh['chan'=32,'wide'=8] {'chan','wide'}, use_global_device_ids=true, to_apply=%region_3.0 | all-reduce | flops 2049 | bytes 16392 | tf_op jit(solution)/shard_map/psum | solution.py:140
  579.3 6.3 all-to-all-done.8
  585.6 17.3 %fusion.6 = f32[2,8,1024]{2,1,0:T(8,128)S(1)} fusion(f32[1024]{0:T(1024)} %copy-done.20, f32[1024]{0:T(1024)} %copy-done.24, f32[2,8,8,128]{3,0,2,1:T(2,128)S(1)} %bitcast.243), kind=kOutput, calls=%fused_computation.10 | convolution fusion | flops 204472320 | bytes 139264 | tf_op jit(solution)/shard_map/xzy,yb->xzb/dot_general | solution.py:123
  605.6 5.3 all-to-all-start.9
  611.0 6.4 all-to-all-done.9
  622.4 5.4 all-to-all-start.10
  627.8 5.9 all-to-all-done.10
  634.9 16.6 %fusion.4 = f32[2,8,1024]{2,1,0:T(8,128)S(1)} fusion(f32[2,8,1024]{2,1,0:T(8,128)S(1)} %all_to_all.251, f32[1024]{0:T(1024)S(1)} %copy-done.22, f32[1024]{0:T(1024)S(1)} %copy-done.26), kind=kOutput, calls=%fused_computation.8 | convolution fusion | flops 204472320 | bytes 139264 | tf_op jit(solution)/shard_map/xzy,yb->xzb/dot_general | solution.py:133
  660.5 7.6 gather_fusion
  698.5 7.5 all-to-all-start.12
  708.1 54.5 %gather_fusion.1 = f32[16384,8]{1,0:T(8,128)} fusion(f32[2049,8]{1,0:T(8,128)S(1)} %concatenate.143, s32[16384]{0:T(1024)S(1)} %copy-done.13), kind=kCustom, calls=%fused_computation.1 | custom fusion | bytes 1114112 | tf_op jit(solution)/shard_map/gather | solution.py:145
  762.6 6.1 copy.126
  771.5 16.8 %fusion.2 = f32[2,8,1024]{2,1,0:T(8,128)S(1)} fusion(f32[1024]{0:T(1024)S(1)} %copy-done.23, f32[1024]{0:T(1024)S(1)} %copy-done.27, f32[2,8,8,128]{3,0,2,1:T(2,128)S(1)} %bitcast.242), kind=kOutput, calls=%fused_computation.6 | convolution fusion | flops 204472320 | bytes 139264 | tf_op jit(solution)/shard_map/xzy,yb->xzb/dot_general | solution.py:123
  806.4 5.2 all-to-all-start.14
  819.0 16.6 %fusion = f32[2,8,1024]{2,1,0:T(8,128)S(1)} fusion(f32[2,8,1024]{2,1,0:T(8,128)S(1)} %all_to_all.267, f32[1024]{0:T(1024)S(1)} %copy-done.23, f32[1024]{0:T(1024)S(1)} %copy-done.27), kind=kOutput, calls=%fused_computation.4 | convolution fusion | flops 204472320 | bytes 139264 | tf_op jit(solution)/shard_map/xzy,yb->xzb/dot_general | solution.py:133
  838.4 7.2 all-to-all-start.15
  846.9 5.5 all-to-all-done.15
  (293 shorter events, 239.1 us)
Async XLA Ops:
  9.0 15.3 %collective-permute-start.24 = (f32[8,1,64,128]{3,2,1,0:T(8,128)S(1)}, f32[8,1,64,128]{3,2,1,0:T(8,128)S(1)}, u32[]{:S(2)}, u32[]{:S(2)}) collective-permute-start(f32[8,1,64,128]{3,2,1,0:T(8,128)S(1)} %get-tuple-element.16), channel_id=1, source_target_pairs={{0,8},{8,16},{16,24},{24,32},{32,40},{40,48},{48,56},{56,64},{64,7... | collective-permute-start | bytes 786440 | tf_op jit(solution)/shard_map/ppermute | solution.py:23
  11.7 11.7 %collective-permute-start.1 = (f32[1,64,128]{2,1,0:T(8,128)S(1)}, f32[1,64,128]{2,1,0:T(8,128)S(1)}, u32[]{:S(2)}, u32[]{:S(2)}) collective-permute-start(f32[1,64,128]{2,1,0:T(8,128)S(1)} %get-tuple-element.56), channel_id=1, source_target_pairs={{0,8},{8,16},{16,24},{24,32},{32,40},{40,48},{48,56},{56,64},{64,7... | collective-permute-start | bytes 98312 | tf_op jit(solution)/shard_map/ppermute | solution.py:23
  15.3 14.6 %collective-permute-start.3 = (f32[1,64,128]{2,1,0:T(8,128)S(1)}, f32[1,64,128]{2,1,0:T(8,128)S(1)}, u32[]{:S(2)}, u32[]{:S(2)}) collective-permute-start(f32[1,64,128]{2,1,0:T(8,128)S(1)} %get-tuple-element.55), channel_id=1, source_target_pairs={{8,0},{16,8},{24,16},{32,24},{40,32},{48,40},{56,48},{64,56},{72,6... | collective-permute-start | bytes 98312 | tf_op jit(solution)/shard_map/ppermute | solution.py:25
  27.9 7.3 collective-permute-start
  35.4 11.8 %collective-permute-start.4 = (f32[4,64,1]{2,1,0:T(8,128)S(1)}, f32[4,64,1]{2,1,0:T(8,128)S(1)}, u32[]{:S(2)}, u32[]{:S(2)}) collective-permute-start(f32[4,64,1]{2,1,0:T(8,128)S(1)} %get-tuple-element.37), channel_id=1, source_target_pairs={{0,1},{1,2},{2,3},{3,4},{4,5},{5,6},{6,7},{8,9},{9,10},{10,11},{11... | collective-permute-start | bytes 3080 | tf_op jit(solution)/shard_map/ppermute | solution.py:23
  39.2 8.0 collective-permute-start.6
  51.3 17.9 %all-to-all-start = ((f32[2,64,128]{2,0,1:T(2,128)}), f32[2,64,128]{2,0,1:T(2,128)S(1)}, u32[]{:S(2)}, u32[]{:S(2)}) async-start(f32[2,64,128]{2,0,1:T(2,128)} %copy.85), calls=%async_computation | async-start | bytes 131072 | tf_op jit(solution)/shard_map/all_to_all | solution.py:122
  88.8 11.3 %all-to-all-start.1 = ((f32[32,1,512]{2,1,0:T(1,128)}), f32[32,1,512]{2,1,0:T(1,128)S(1)}, u32[]{:S(2)}, u32[]{:S(2)}) async-start(f32[32,1,512]{2,1,0:T(1,128)} %reshape.171), calls=%async_computation.1 | async-start | bytes 131072 | tf_op jit(solution)/shard_map/all_to_all | solution.py:124
  152.3 7.3 collective-permute-start.8
  202.2 10.4 %all-to-all-start.5 = ((f32[32,1,512]{2,1,0:T(1,128)}), f32[32,1,512]{2,1,0:T(1,128)S(1)}, u32[]{:S(2)}, u32[]{:S(2)}) async-start(f32[32,1,512]{2,1,0:T(1,128)} %reshape.177), calls=%async_computation.5 | async-start | bytes 131072 | tf_op jit(solution)/shard_map/all_to_all | solution.py:124
  206.3 470.3 %collective-permute-start.25 = (f32[8,1,64,128]{3,2,1,0:T(8,128)}, f32[8,1,64,128]{3,2,1,0:T(8,128)}, u32[]{:S(2)}, u32[]{:S(2)}) collective-permute-start(f32[8,1,64,128]{3,2,1,0:T(8,128)} %get-tuple-element.15), channel_id=1, source_target_pairs={{8,0},{16,8},{24,16},{32,24},{40,32},{48,40},{56,48},{64,56},{72,6... | collective-permute-start | bytes 786440 | tf_op jit(solution)/shard_map/ppermute | solution.py:25
  217.6 121.0 %all-to-all-start.6 = ((f32[32,1,512]{2,1,0:T(1,128)}), f32[32,1,512]{2,1,0:T(1,128)S(1)}, u32[]{:S(2)}, u32[]{:S(2)}) async-start(f32[32,1,512]{2,1,0:T(1,128)} %reshape.179), calls=%async_computation.6 | async-start | bytes 131072 | tf_op jit(solution)/shard_map/all_to_all | solution.py:132
  222.6 436.3 %all-reduce.8.cloned.1.call-start = ((), (), s32[]{:S(2)}) async-start(), calls=%async_computation.16 | async-start | bytes 2105344 | tf_op jit(solution)/shard_map/psum | solution.py:140
  359.3 10.9 %all-to-all-start.7 = ((f32[8,1,2048]{2,1,0:T(1,128)}), f32[8,1,2048]{2,1,0:T(1,128)S(1)}, u32[]{:S(2)}, u32[]{:S(2)}) async-start(f32[8,1,2048]{2,1,0:T(1,128)} %reshape.181), calls=%async_computation.7 | async-start | bytes 131072 | tf_op jit(solution)/shard_map/all_to_all | solution.py:134
  373.4 114.7 %collective-permute-start.13 = (f32[1,64,128]{2,1,0:T(8,128)S(1)}, f32[1,64,128]{2,1,0:T(8,128)S(1)}, u32[]{:S(2)}, u32[]{:S(2)}) collective-permute-start(f32[1,64,128]{2,1,0:T(8,128)S(1)} %get-tuple-element.50), channel_id=1, source_target_pairs={{8,0},{16,8},{24,16},{32,24},{40,32},{48,40},{56,48},{64,56},{72,6... | collective-permute-start | bytes 98312 | tf_op jit(solution)/shard_map/ppermute | solution.py:25
  375.9 112.3 %collective-permute-start.12 = (f32[1,64,128]{2,1,0:T(8,128)S(1)}, f32[1,64,128]{2,1,0:T(8,128)S(1)}, u32[]{:S(2)}, u32[]{:S(2)}) collective-permute-start(f32[1,64,128]{2,1,0:T(8,128)S(1)} %get-tuple-element.49), channel_id=1, source_target_pairs={{0,8},{8,16},{16,24},{24,32},{32,40},{40,48},{48,56},{56,64},{64,7... | collective-permute-start | bytes 98312 | tf_op jit(solution)/shard_map/ppermute | solution.py:23
  488.3 85.6 %collective-permute-start.15 = (f32[4,64,1]{2,1,0:T(8,128)S(1)}, f32[4,64,1]{2,1,0:T(8,128)S(1)}, u32[]{:S(2)}, u32[]{:S(2)}) collective-permute-start(f32[4,64,1]{2,1,0:T(8,128)S(1)} %get-tuple-element.30), channel_id=1, source_target_pairs={{1,0},{2,1},{3,2},{4,3},{5,4},{6,5},{7,6},{9,8},{10,9},{11,10},{12... | collective-permute-start | bytes 3080 | tf_op jit(solution)/shard_map/ppermute | solution.py:25
  490.6 83.2 %collective-permute-start.14 = (f32[4,64,1]{2,1,0:T(8,128)S(1)}, f32[4,64,1]{2,1,0:T(8,128)S(1)}, u32[]{:S(2)}, u32[]{:S(2)}) collective-permute-start(f32[4,64,1]{2,1,0:T(8,128)S(1)} %get-tuple-element.29), channel_id=1, source_target_pairs={{0,1},{1,2},{2,3},{3,4},{4,5},{5,6},{6,7},{8,9},{9,10},{10,11},{11... | collective-permute-start | bytes 3080 | tf_op jit(solution)/shard_map/ppermute | solution.py:23
  575.0 10.5 %all-to-all-start.8 = ((f32[2,64,128]{2,0,1:T(2,128)}), f32[2,64,128]{2,0,1:T(2,128)S(1)}, u32[]{:S(2)}, u32[]{:S(2)}) async-start(f32[2,64,128]{2,0,1:T(2,128)} %copy.103), calls=%async_computation.8 | async-start | bytes 131072 | tf_op jit(solution)/shard_map/all_to_all | solution.py:122
  605.6 11.8 %all-to-all-start.9 = ((f32[32,1,512]{2,1,0:T(1,128)}), f32[32,1,512]{2,1,0:T(1,128)S(1)}, u32[]{:S(2)}, u32[]{:S(2)}) async-start(f32[32,1,512]{2,1,0:T(1,128)} %reshape.183), calls=%async_computation.9 | async-start | bytes 131072 | tf_op jit(solution)/shard_map/all_to_all | solution.py:124
  622.4 11.4 %all-to-all-start.10 = ((f32[32,1,512]{2,1,0:T(1,128)}), f32[32,1,512]{2,1,0:T(1,128)S(1)}, u32[]{:S(2)}, u32[]{:S(2)}) async-start(f32[32,1,512]{2,1,0:T(1,128)} %reshape.185), calls=%async_computation.10 | async-start | bytes 131072 | tf_op jit(solution)/shard_map/all_to_all | solution.py:132
  654.2 13.9 %all-to-all-start.11 = ((f32[8,1,2048]{2,1,0:T(1,128)}), f32[8,1,2048]{2,1,0:T(1,128)S(1)}, u32[]{:S(2)}, u32[]{:S(2)}) async-start(f32[8,1,2048]{2,1,0:T(1,128)} %reshape.187), calls=%async_computation.11 | async-start | bytes 131072 | tf_op jit(solution)/shard_map/all_to_all | solution.py:134
  674.7 7.3 collective-permute-start.16
  682.8 13.6 %collective-permute-start.19 = (f32[4,64,1]{2,1,0:T(8,128)}, f32[4,64,1]{2,1,0:T(8,128)}, u32[]{:S(2)}, u32[]{:S(2)}) collective-permute-start(f32[4,64,1]{2,1,0:T(8,128)} %get-tuple-element.28), channel_id=1, source_target_pairs={{1,0},{2,1},{3,2},{4,3},{5,4},{6,5},{7,6},{9,8},{10,9},{11,10},{12... | collective-permute-start | bytes 3080 | tf_op jit(solution)/shard_map/ppermute | solution.py:25
  685.2 11.2 %collective-permute-start.18 = (f32[4,64,1]{2,1,0:T(8,128)}, f32[4,64,1]{2,1,0:T(8,128)}, u32[]{:S(2)}, u32[]{:S(2)}) collective-permute-start(f32[4,64,1]{2,1,0:T(8,128)} %get-tuple-element.27), channel_id=1, source_target_pairs={{0,1},{1,2},{2,3},{3,4},{4,5},{5,6},{6,7},{8,9},{9,10},{10,11},{11... | collective-permute-start | bytes 3080 | tf_op jit(solution)/shard_map/ppermute | solution.py:23
  690.0 78.6 %collective-permute-start.27 = (f32[8,4,64,1]{2,0,3,1:T(8,128)}, f32[8,4,64,1]{2,0,3,1:T(8,128)S(1)}, u32[]{:S(2)}, u32[]{:S(2)}) collective-permute-start(f32[8,4,64,1]{2,0,3,1:T(8,128)} %copy.122), channel_id=1, source_target_pairs={{1,0},{2,1},{3,2},{4,3},{5,4},{6,5},{7,6},{9,8},{10,9},{11,10},{12... | collective-permute-start | bytes 24584 | tf_op jit(solution)/shard_map/ppermute | solution.py:25
  693.5 76.6 %collective-permute-start.26 = (f32[8,4,64,1]{2,0,3,1:T(8,128)S(1)}, f32[8,4,64,1]{2,0,3,1:T(8,128)S(1)}, u32[]{:S(2)}, u32[]{:S(2)}) collective-permute-start(f32[8,4,64,1]{2,0,3,1:T(8,128)S(1)} %copy.121), channel_id=1, source_target_pairs={{0,1},{1,2},{2,3},{3,4},{4,5},{5,6},{6,7},{8,9},{9,10},{10,11},{11... | collective-permute-start | bytes 24584 | tf_op jit(solution)/shard_map/ppermute | solution.py:23
  698.5 72.9 %all-to-all-start.12 = ((f32[2,64,128]{2,0,1:T(2,128)}), f32[2,64,128]{2,0,1:T(2,128)S(1)}, u32[]{:S(2)}, u32[]{:S(2)}) async-start(f32[2,64,128]{2,0,1:T(2,128)} %copy.112), calls=%async_computation.12 | async-start | bytes 131072 | tf_op jit(solution)/shard_map/all_to_all | solution.py:122
  791.0 10.5 %all-to-all-start.13 = ((f32[32,1,512]{2,1,0:T(1,128)}), f32[32,1,512]{2,1,0:T(1,128)S(1)}, u32[]{:S(2)}, u32[]{:S(2)}) async-start(f32[32,1,512]{2,1,0:T(1,128)} %reshape.189), calls=%async_computation.13 | async-start | bytes 131072 | tf_op jit(solution)/shard_map/all_to_all | solution.py:124
  806.4 11.4 %all-to-all-start.14 = ((f32[32,1,512]{2,1,0:T(1,128)}), f32[32,1,512]{2,1,0:T(1,128)S(1)}, u32[]{:S(2)}, u32[]{:S(2)}) async-start(f32[32,1,512]{2,1,0:T(1,128)} %reshape.191), calls=%async_computation.14 | async-start | bytes 131072 | tf_op jit(solution)/shard_map/all_to_all | solution.py:132
  838.4 14.1 %all-to-all-start.15 = ((f32[8,1,2048]{2,1,0:T(1,128)}), f32[8,1,2048]{2,1,0:T(1,128)S(1)}, u32[]{:S(2)}, u32[]{:S(2)}) async-start(f32[8,1,2048]{2,1,0:T(1,128)} %reshape.193), calls=%async_computation.15 | async-start | bytes 131072 | tf_op jit(solution)/shard_map/all_to_all | solution.py:134
  859.9 7.3 collective-permute-start.20
  (41 other events, 2203.3 us)
Sparse Core Ops, SparseCore 0:
  338.7 255.6 all-reduce.7
where the time goes:
time: 900 us; the launch traced here: 888 us
  other arithmetic  249 us (28%)
  starting transfers between devices  150 us (17%)
  matrix products  142 us (16%)
  local copies, waits for them, and re-layouts  132 us (15%)
  blocking collectives  114 us (13%)
  waiting for transfers between devices  86 us (10%)
  between operations  16 us (2%)
    scatter-add x1, other arithmetic, per_device(): jax.ops.segment_sum(cell_rows, owners, num_segments=junction_total + 1)  110 us
    scatter-add x1, other arithmetic, per_device(): jax.ops.segment_sum(jnp.ones(owners.shape, jnp.float32), owners, num_segm...  110 us
    psum x1, blocking collectives, per_device(): lax.psum((junction_sums, cell_counts), ('chan', 'wide'))  79.7 us
    dot_general x4, matrix products, per_device(): across = jnp.einsum('xzy,yb->xzb', spectrum, table_y, precision=highest)  67.5 us
    dot_general x4, matrix products, per_device(): spectrum = jnp.einsum('xzy,yb->xzb', across, table_y, precision=highest)  66.6 us
    gather x1, local copies, waits for them, and re-layouts, per_device(): source = table[owners].T.reshape(concs.shape)  54.5 us
    ppermute x14, starting transfers between devices, with_halo(): lax.ppermute(head, axis, [((i + 1) % count, i) for i in range(ends)])  39.7 us
    ppermute x14, starting transfers between devices, with_halo(): lax.ppermute(tail, axis, [(i, (i + 1) % count) for i in range(ends)])  37.9 us
  transfers between devices with their start and end apart: 42, of which 20 were waited for; matrix products, arithmetic and copies ran while one was open for 45% of the time, Pallas kernels for 0%

commit v1 on v0

--- a/solution.py
+++ b/solution.py
@@ -137,7 +137,8 @@
         )
     cell_rows = concs.reshape(species_all, -1).T
     junction_sums = jax.ops.segment_sum(cell_rows, owners, num_segments=junction_total + 1)
-    junction_sums, total_counts = lax.psum((junction_sums, cell_counts), ("chan", "wide"))
+    vector_play = lambda sample: lax.psum(lax.psum(sample, axis_name="chan"), axis_name="wide")
+    junction_sums, total_counts = vector_play((junction_sums, cell_counts))
     means = junction_sums / jnp.maximum(total_counts, 1.0)[:, None]
     own_means = means[:junction_total]
     table = coupling * (own_means[partner] - own_means)

time: 900 us -> 1020 us (1.13)
  blocking collectives: 114 us -> 177 us
  waiting for transfers between devices: 86 us -> 124 us
  starting transfers between devices: 150 us -> 170 us
    psum x1 -> x2, blocking collectives: 79.7 us -> 132 us  [the longest x1 104 us: per_device(): lax.psum(sample, axis_name='chan')]
    psum x1 -> x2, waiting for transfers between devices: 0.01 us -> 47 us  [the longest x1 46.9 us: per_device(): lax.psum(lax.psum(sample, axis_name='chan'), axis_name='wide')]
    all_to_all x4 -> x3, starting transfers between devices: 18.6 us -> 32.1 us  [per_device(): lax.all_to_all(across, 'chan', split_axis=2, concat_axis=0, tiled=True)]
    all_to_all x0 -> x1, blocking collectives: none -> 10.2 us  [per_device(): lax.all_to_all(across, 'chan', split_axis=2, concat_axis=0, tiled=True)]
    unnamed x89 -> x91, local copies, waits for them, and re-layouts: 34.9 us -> 34.3 us
  transfers between devices with their start and end apart: 42 -> 42, of which waited for: 20 -> 21; matrix products, arithmetic and copies ran while one was open for 45% -> 39% of each run, Pallas kernels for 0% -> 0%
where the time goes in v1:
time: 1020 us; the launch traced here: 1010 us
  other arithmetic  248 us (24%)
  blocking collectives  177 us (17%)
  starting transfers between devices  170 us (17%)
  matrix products  142 us (14%)
  local copies, waits for them, and re-layouts  131 us (13%)
  waiting for transfers between devices  124 us (12%)
  between operations  16 us (2%)
    scatter-add x1, other arithmetic, per_device(): jax.ops.segment_sum(cell_rows, owners, num_segments=junction_total + 1)  110 us
    scatter-add x1, other arithmetic, per_device(): jax.ops.segment_sum(jnp.ones(owners.shape, jnp.float32), owners, num_segm...  110 us
    psum x1, blocking collectives, per_device(): lax.psum(sample, axis_name='chan')  104 us
    dot_general x4, matrix products, per_device(): across = jnp.einsum('xzy,yb->xzb', spectrum, table_y, precision=highest)  67.5 us
    dot_general x4, matrix products, per_device(): spectrum = jnp.einsum('xzy,yb->xzb', across, table_y, precision=highest)  66.6 us
    gather x1, local copies, waits for them, and re-layouts, per_device(): source = table[owners].T.reshape(concs.shape)  54.5 us
    psum x1, waiting for transfers between devices, per_device(): lax.psum(lax.psum(sample, axis_name='chan'), axis_name='wide')  46.9 us
    ppermute x14, starting transfers between devices, with_halo(): lax.ppermute(tail, axis, [(i, (i + 1) % count) for i in range(ends)])  38.6 us
  transfers between devices with their start and end apart: 42, of which 21 were waited for; matrix products, arithmetic and copies ran while one was open for 39% of the time, Pallas kernels for 0%

profile of v1, /device:TPU:34, one launch (start us, length us, event | category | flops | bytes accessed | tf_op | source)
XLA Modules:
  0.0 1007.5 jit_solution(16215715711538498263)
XLA Ops:
  51.3 11.0 %all-to-all-start = ((f32[2,64,128]{2,0,1:T(2,128)}), f32[2,64,128]{2,0,1:T(2,128)S(1)}, u32[]{:S(2)}, u32[]{:S(2)}) async-start(f32[2,64,128]{2,0,1:T(2,128)} %copy.85), calls=%async_computation | async-start | bytes 131072 | tf_op jit(solution)/shard_map/all_to_all | solution.py:122
  62.4 6.8 all-to-all-done
  69.2 16.6 %fusion.14 = f32[2,8,1024]{2,1,0:T(8,128)S(1)} fusion(f32[1024]{0:T(1024)S(1)} %get-tuple-element.64, f32[1024]{0:T(1024)S(1)} %get-tuple-element.65, f32[2,8,8,128]{3,0,2,1:T(2,128)S(1)} %bitcast.241), kind=kOutput, calls=%fused_computation.18 | convolution fusion | flops 204472320 | bytes 139264 | tf_op jit(solution)/shard_map/xzy,yb->xzb/dot_general | solution.py:123
  93.7 6.2 all-to-all-done.1
  104.8 10.9 %all_to_all.288 = f32[32,1,512]{2,1,0:T(1,128)S(1)} all-to-all(f32[32,1,512]{2,1,0:T(1,128)S(1)} %reshape.173), channel_id=1, replica_groups=mesh['chan'=32,'wide'=8] {'chan'}, dimensions={0} | all-to-all | bytes 131072 | tf_op jit(solution)/shard_map/all_to_all | solution.py:132
  116.8 16.6 %fusion.12 = f32[2,8,1024]{2,1,0:T(8,128)S(1)} fusion(f32[2,8,1024]{2,1,0:T(8,128)S(1)} %all_to_all.219, f32[1024]{0:T(1024)S(1)} %get-tuple-element.64, f32[1024]{0:T(1024)S(1)} %get-tuple-element.65), kind=kOutput, calls=%fused_computation.16 | convolution fusion | flops 204472320 | bytes 139264 | tf_op jit(solution)/shard_map/xzy,yb->xzb/dot_general | solution.py:133
  135.5 10.8 %all_to_all.289 = f32[8,1,2048]{2,1,0:T(1,128)S(1)} all-to-all(f32[8,1,2048]{2,1,0:T(1,128)S(1)} %reshape.175), channel_id=1, replica_groups=mesh['chan'=32,'wide'=8] {'wide'}, dimensions={0} | all-to-all | bytes 131072 | tf_op jit(solution)/shard_map/all_to_all | solution.py:134
  153.9 5.4 collective-permute-done.8
  170.1 12.4 %all_to_all.290 = f32[2,64,128]{2,0,1:T(2,128)S(1)} all-to-all(f32[2,64,128]{2,0,1:T(2,128)S(1)} %copy.94), channel_id=1, replica_groups=mesh['chan'=32,'wide'=8] {'wide'}, dimensions={1} | all-to-all | bytes 131072 | tf_op jit(solution)/shard_map/all_to_all | solution.py:122
  182.6 16.8 %fusion.10 = f32[2,8,1024]{2,1,0:T(8,128)S(1)} fusion(f32[1024]{0:T(1024)S(1)} %get-tuple-element.64, f32[1024]{0:T(1024)S(1)} %get-tuple-element.65, f32[2,8,8,128]{3,0,2,1:T(2,128)S(1)} %bitcast.244), kind=kOutput, calls=%fused_computation.14 | convolution fusion | flops 204472320 | bytes 139264 | tf_op jit(solution)/shard_map/xzy,yb->xzb/dot_general | solution.py:123
  201.5 10.2 %all_to_all.291 = f32[32,1,512]{2,1,0:T(1,128)S(1)} all-to-all(f32[32,1,512]{2,1,0:T(1,128)S(1)} %reshape.177), channel_id=1, replica_groups=mesh['chan'=32,'wide'=8] {'chan'}, dimensions={0} | all-to-all | bytes 131072 | tf_op jit(solution)/shard_map/all_to_all | solution.py:124
  232.0 16.8 %fusion.8 = f32[2,8,1024]{2,1,0:T(8,128)S(1)} fusion(f32[2,8,1024]{2,1,0:T(8,128)S(1)} %all_to_all.235, f32[1024]{0:T(1024)S(1)} %copy-done.22, f32[1024]{0:T(1024)S(1)} %copy-done.26), kind=kOutput, calls=%fused_computation.12 | convolution fusion | flops 204472320 | bytes 139264 | tf_op jit(solution)/shard_map/xzy,yb->xzb/dot_general | solution.py:133
  256.4 110.2 %scatter_custom_fusion = f32[2049,8]{1,0:T(8,128)} fusion(s32[16384]{0:T(1024)S(1)} %bitcast.237, f32[16384,8]{1,0:T(8,128)} %bitcast.196, f32[]{:T(128)} %constant.28.clone.1), kind=kCustom, calls=%fused_computation.84 | custom fusion | flops 131072 | bytes 66080 | tf_op jit(solution)/shard_map/scatter-add | solution.py:139
  389.1 9.3 all-to-all-start.8
  399.0 109.7 %scatter_custom_fusion.1 = f32[2049]{0:T(1024)S(1)} fusion(s32[16384]{0:T(1024)S(1)} %bitcast.239, f32[16384]{0:T(1024)S(1)} %broadcast.172, f32[]{:T(128)} %constant.28.clone.1), kind=kCustom, calls=%fused_computation.420 | custom fusion | flops 16384 | bytes 8200 | tf_op jit(solution)/shard_map/scatter-add | solution.py:104
  508.8 104.4 %psum.30 = f32[2049]{0:T(1024)S(1)} all-reduce(f32[2049]{0:T(1024)S(1)} %scatter_custom_fusion.1), channel_id=1, replica_groups=mesh['chan'=32,'wide'=8] {'chan'}, use_global_device_ids=true, to_apply=%region_4.5 | all-reduce | flops 2049 | bytes 16392 | tf_op jit(solution)/shard_map/psum | solution.py:140
  613.2 28.0 %psum.31 = f32[2049]{0:T(1024)S(1)} all-reduce(f32[2049]{0:T(1024)S(1)} %psum.30), channel_id=1, replica_groups=mesh['chan'=32,'wide'=8] {'wide'}, use_global_device_ids=true, to_apply=%region_5.6 | all-reduce | flops 2049 | bytes 16392 | tf_op jit(solution)/shard_map/psum | solution.py:140
  641.2 17.3 %fusion.6 = f32[2,8,1024]{2,1,0:T(8,128)S(1)} fusion(f32[1024]{0:T(1024)} %copy-done.21, f32[1024]{0:T(1024)} %copy-done.25, f32[2,8,8,128]{3,0,2,1:T(2,128)S(1)} %bitcast.243), kind=kOutput, calls=%fused_computation.10 | convolution fusion | flops 204472320 | bytes 139264 | tf_op jit(solution)/shard_map/xzy,yb->xzb/dot_general | solution.py:123
  661.3 21.8 %all-to-all-start.9 = ((f32[32,1,512]{2,1,0:T(1,128)}), f32[32,1,512]{2,1,0:T(1,128)S(1)}, u32[]{:S(2)}, u32[]{:S(2)}) async-start(f32[32,1,512]{2,1,0:T(1,128)} %reshape.183), calls=%async_computation.9 | async-start | bytes 131072 | tf_op jit(solution)/shard_map/all_to_all | solution.py:124
  683.1 6.4 all-to-all-done.9
  700.1 5.6 all-to-all-done.10
  707.0 16.6 %fusion.4 = f32[2,8,1024]{2,1,0:T(8,128)S(1)} fusion(f32[2,8,1024]{2,1,0:T(8,128)S(1)} %all_to_all.251, f32[1024]{0:T(1024)S(1)} %copy-done.23, f32[1024]{0:T(1024)S(1)} %copy-done.27), kind=kOutput, calls=%fused_computation.8 | convolution fusion | flops 204472320 | bytes 139264 | tf_op jit(solution)/shard_map/xzy,yb->xzb/dot_general | solution.py:133
  726.3 6.2 all-to-all-start.11
  732.5 46.9 %all-reduce.11.cloned.1.call-done = f32[2049,8]{1,0:T(8,128)} async-done(((f32[2049,8]{1,0:T(8,128)}), f32[2049,8]{1,0:T(8,128)}) %all-reduce.11.cloned.1.call-update) | async-done | bytes 65584 | tf_op jit(solution)/shard_map/psum | solution.py:140
  781.0 7.6 gather_fusion
  817.6 7.1 all-to-all-start.12
  826.7 54.5 %gather_fusion.1 = f32[16384,8]{1,0:T(8,128)} fusion(f32[2049,8]{1,0:T(8,128)S(1)} %concatenate.143, s32[16384]{0:T(1024)S(1)} %copy-done.13), kind=kCustom, calls=%fused_computation.1 | custom fusion | bytes 1114112 | tf_op jit(solution)/shard_map/gather | solution.py:146
  881.2 6.1 copy.126
  890.1 16.8 %fusion.2 = f32[2,8,1024]{2,1,0:T(8,128)S(1)} fusion(f32[1024]{0:T(1024)S(1)} %copy-done.24, f32[1024]{0:T(1024)S(1)} %copy-done.28, f32[2,8,8,128]{3,0,2,1:T(2,128)S(1)} %bitcast.242), kind=kOutput, calls=%fused_computation.6 | convolution fusion | flops 204472320 | bytes 139264 | tf_op jit(solution)/shard_map/xzy,yb->xzb/dot_general | solution.py:123
  938.8 16.6 %fusion = f32[2,8,1024]{2,1,0:T(8,128)S(1)} fusion(f32[2,8,1024]{2,1,0:T(8,128)S(1)} %all_to_all.267, f32[1024]{0:T(1024)S(1)} %copy-done.24, f32[1024]{0:T(1024)S(1)} %copy-done.28), kind=kOutput, calls=%fused_computation.4 | convolution fusion | flops 204472320 | bytes 139264 | tf_op jit(solution)/shard_map/xzy,yb->xzb/dot_general | solution.py:133
  958.1 7.2 all-to-all-start.15
  966.7 5.5 all-to-all-done.15
  (298 shorter events, 247.0 us)
Async XLA Ops:
  9.0 15.3 %collective-permute-start.24 = (f32[8,1,64,128]{3,2,1,0:T(8,128)S(1)}, f32[8,1,64,128]{3,2,1,0:T(8,128)S(1)}, u32[]{:S(2)}, u32[]{:S(2)}) collective-permute-start(f32[8,1,64,128]{3,2,1,0:T(8,128)S(1)} %get-tuple-element.16), channel_id=1, source_target_pairs={{0,8},{8,16},{16,24},{24,32},{32,40},{40,48},{48,56},{56,64},{64,7... | collective-permute-start | bytes 786440 | tf_op jit(solution)/shard_map/ppermute | solution.py:23
  11.7 11.7 %collective-permute-start.1 = (f32[1,64,128]{2,1,0:T(8,128)S(1)}, f32[1,64,128]{2,1,0:T(8,128)S(1)}, u32[]{:S(2)}, u32[]{:S(2)}) collective-permute-start(f32[1,64,128]{2,1,0:T(8,128)S(1)} %get-tuple-element.56), channel_id=1, source_target_pairs={{0,8},{8,16},{16,24},{24,32},{32,40},{40,48},{48,56},{56,64},{64,7... | collective-permute-start | bytes 98312 | tf_op jit(solution)/shard_map/ppermute | solution.py:23
  15.3 14.6 %collective-permute-start.3 = (f32[1,64,128]{2,1,0:T(8,128)S(1)}, f32[1,64,128]{2,1,0:T(8,128)S(1)}, u32[]{:S(2)}, u32[]{:S(2)}) collective-permute-start(f32[1,64,128]{2,1,0:T(8,128)S(1)} %get-tuple-element.55), channel_id=1, source_target_pairs={{8,0},{16,8},{24,16},{32,24},{40,32},{48,40},{56,48},{64,56},{72,6... | collective-permute-start | bytes 98312 | tf_op jit(solution)/shard_map/ppermute | solution.py:25
  27.9 7.3 collective-permute-start
  35.4 11.8 %collective-permute-start.4 = (f32[4,64,1]{2,1,0:T(8,128)S(1)}, f32[4,64,1]{2,1,0:T(8,128)S(1)}, u32[]{:S(2)}, u32[]{:S(2)}) collective-permute-start(f32[4,64,1]{2,1,0:T(8,128)S(1)} %get-tuple-element.37), channel_id=1, source_target_pairs={{0,1},{1,2},{2,3},{3,4},{4,5},{5,6},{6,7},{8,9},{9,10},{10,11},{11... | collective-permute-start | bytes 3080 | tf_op jit(solution)/shard_map/ppermute | solution.py:23
  39.2 8.0 collective-permute-start.6
  41.4 6.9 collective-permute-start.7
  43.3 6.9 collective-permute-start.5
  51.3 17.9 %all-to-all-start = ((f32[2,64,128]{2,0,1:T(2,128)}), f32[2,64,128]{2,0,1:T(2,128)S(1)}, u32[]{:S(2)}, u32[]{:S(2)}) async-start(f32[2,64,128]{2,0,1:T(2,128)} %copy.85), calls=%async_computation | async-start | bytes 131072 | tf_op jit(solution)/shard_map/all_to_all | solution.py:122
  88.6 11.3 %all-to-all-start.1 = ((f32[32,1,512]{2,1,0:T(1,128)}), f32[32,1,512]{2,1,0:T(1,128)S(1)}, u32[]{:S(2)}, u32[]{:S(2)}) async-start(f32[32,1,512]{2,1,0:T(1,128)} %reshape.171), calls=%async_computation.1 | async-start | bytes 131072 | tf_op jit(solution)/shard_map/all_to_all | solution.py:124
  152.0 7.3 collective-permute-start.8
  159.4 6.9 collective-permute-start.11
  216.7 14.1 %all-to-all-start.6 = ((f32[32,1,512]{2,1,0:T(1,128)}), f32[32,1,512]{2,1,0:T(1,128)S(1)}, u32[]{:S(2)}, u32[]{:S(2)}) async-start(f32[32,1,512]{2,1,0:T(1,128)} %reshape.179), calls=%async_computation.6 | async-start | bytes 131072 | tf_op jit(solution)/shard_map/all_to_all | solution.py:132
  221.7 574.5 %collective-permute-start.25 = (f32[8,1,64,128]{3,2,1,0:T(8,128)}, f32[8,1,64,128]{3,2,1,0:T(8,128)}, u32[]{:S(2)}, u32[]{:S(2)}) collective-permute-start(f32[8,1,64,128]{3,2,1,0:T(8,128)} %get-tuple-element.15), channel_id=1, source_target_pairs={{8,0},{16,8},{24,16},{32,24},{40,32},{48,40},{56,48},{64,56},{72,6... | collective-permute-start | bytes 786440 | tf_op jit(solution)/shard_map/ppermute | solution.py:25
  251.6 114.9 %all-to-all-start.7 = ((f32[8,1,2048]{2,1,0:T(1,128)}), f32[8,1,2048]{2,1,0:T(1,128)S(1)}, u32[]{:S(2)}, u32[]{:S(2)}) async-start(f32[8,1,2048]{2,1,0:T(1,128)} %reshape.181), calls=%async_computation.7 | async-start | bytes 131072 | tf_op jit(solution)/shard_map/all_to_all | solution.py:134
  256.3 443.6 %all-reduce.9.cloned.1.call-start = ((), (), s32[]{:S(2)}) async-start(), calls=%async_computation.16 | async-start | bytes 2105344 | tf_op jit(solution)/shard_map/psum | solution.py:140
  371.7 7.3 collective-permute-start.12
  389.1 252.1 %all-to-all-start.8 = ((f32[2,64,128]{2,0,1:T(2,128)}), f32[2,64,128]{2,0,1:T(2,128)S(1)}, u32[]{:S(2)}, u32[]{:S(2)}) async-start(f32[2,64,128]{2,0,1:T(2,128)} %copy.103), calls=%async_computation.8 | async-start | bytes 131072 | tf_op jit(solution)/shard_map/all_to_all | solution.py:122
  661.3 28.2 %all-to-all-start.9 = ((f32[32,1,512]{2,1,0:T(1,128)}), f32[32,1,512]{2,1,0:T(1,128)S(1)}, u32[]{:S(2)}, u32[]{:S(2)}) async-start(f32[32,1,512]{2,1,0:T(1,128)} %reshape.183), calls=%async_computation.9 | async-start | bytes 131072 | tf_op jit(solution)/shard_map/all_to_all | solution.py:124
  694.4 11.4 %all-to-all-start.10 = ((f32[32,1,512]{2,1,0:T(1,128)}), f32[32,1,512]{2,1,0:T(1,128)S(1)}, u32[]{:S(2)}, u32[]{:S(2)}) async-start(f32[32,1,512]{2,1,0:T(1,128)} %reshape.185), calls=%async_computation.10 | async-start | bytes 131072 | tf_op jit(solution)/shard_map/all_to_all | solution.py:132
  699.4 80.1 %all-reduce.11.cloned.1.call-start = ((), (), s32[]{:S(2)}) async-start(), calls=%async_computation.17 | async-start | bytes 2105344 | tf_op jit(solution)/shard_map/psum | solution.py:140
  726.3 62.4 %all-to-all-start.11 = ((f32[8,1,2048]{2,1,0:T(1,128)}), f32[8,1,2048]{2,1,0:T(1,128)S(1)}, u32[]{:S(2)}, u32[]{:S(2)}) async-start(f32[8,1,2048]{2,1,0:T(1,128)} %reshape.187), calls=%async_computation.11 | async-start | bytes 131072 | tf_op jit(solution)/shard_map/all_to_all | solution.py:134
  793.8 7.3 collective-permute-start.16
  801.9 13.6 %collective-permute-start.19 = (f32[4,64,1]{2,1,0:T(8,128)}, f32[4,64,1]{2,1,0:T(8,128)}, u32[]{:S(2)}, u32[]{:S(2)}) collective-permute-start(f32[4,64,1]{2,1,0:T(8,128)} %get-tuple-element.28), channel_id=1, source_target_pairs={{1,0},{2,1},{3,2},{4,3},{5,4},{6,5},{7,6},{9,8},{10,9},{11,10},{12... | collective-permute-start | bytes 3080 | tf_op jit(solution)/shard_map/ppermute | solution.py:25
  804.7 10.9 %collective-permute-start.18 = (f32[4,64,1]{2,1,0:T(8,128)}, f32[4,64,1]{2,1,0:T(8,128)}, u32[]{:S(2)}, u32[]{:S(2)}) collective-permute-start(f32[4,64,1]{2,1,0:T(8,128)} %get-tuple-element.27), channel_id=1, source_target_pairs={{0,1},{1,2},{2,3},{3,4},{4,5},{5,6},{6,7},{8,9},{9,10},{10,11},{11... | collective-permute-start | bytes 3080 | tf_op jit(solution)/shard_map/ppermute | solution.py:23
  809.2 78.1 %collective-permute-start.27 = (f32[8,4,64,1]{2,0,3,1:T(8,128)}, f32[8,4,64,1]{2,0,3,1:T(8,128)S(1)}, u32[]{:S(2)}, u32[]{:S(2)}) collective-permute-start(f32[8,4,64,1]{2,0,3,1:T(8,128)} %copy.122), channel_id=1, source_target_pairs={{1,0},{2,1},{3,2},{4,3},{5,4},{6,5},{7,6},{9,8},{10,9},{11,10},{12... | collective-permute-start | bytes 24584 | tf_op jit(solution)/shard_map/ppermute | solution.py:25
  813.0 75.7 %collective-permute-start.26 = (f32[8,4,64,1]{2,0,3,1:T(8,128)S(1)}, f32[8,4,64,1]{2,0,3,1:T(8,128)S(1)}, u32[]{:S(2)}, u32[]{:S(2)}) collective-permute-start(f32[8,4,64,1]{2,0,3,1:T(8,128)S(1)} %copy.121), channel_id=1, source_target_pairs={{0,1},{1,2},{2,3},{3,4},{4,5},{5,6},{6,7},{8,9},{9,10},{10,11},{11... | collective-permute-start | bytes 24584 | tf_op jit(solution)/shard_map/ppermute | solution.py:23
  817.6 72.4 %all-to-all-start.12 = ((f32[2,64,128]{2,0,1:T(2,128)}), f32[2,64,128]{2,0,1:T(2,128)S(1)}, u32[]{:S(2)}, u32[]{:S(2)}) async-start(f32[2,64,128]{2,0,1:T(2,128)} %copy.112), calls=%async_computation.12 | async-start | bytes 131072 | tf_op jit(solution)/shard_map/all_to_all | solution.py:122
  909.6 11.6 %all-to-all-start.13 = ((f32[32,1,512]{2,1,0:T(1,128)}), f32[32,1,512]{2,1,0:T(1,128)S(1)}, u32[]{:S(2)}, u32[]{:S(2)}) async-start(f32[32,1,512]{2,1,0:T(1,128)} %reshape.189), calls=%async_computation.13 | async-start | bytes 131072 | tf_op jit(solution)/shard_map/all_to_all | solution.py:124
  926.2 11.4 %all-to-all-start.14 = ((f32[32,1,512]{2,1,0:T(1,128)}), f32[32,1,512]{2,1,0:T(1,128)S(1)}, u32[]{:S(2)}, u32[]{:S(2)}) async-start(f32[32,1,512]{2,1,0:T(1,128)} %reshape.191), calls=%async_computation.14 | async-start | bytes 131072 | tf_op jit(solution)/shard_map/all_to_all | solution.py:132
  958.1 14.1 %all-to-all-start.15 = ((f32[8,1,2048]{2,1,0:T(1,128)}), f32[8,1,2048]{2,1,0:T(1,128)S(1)}, u32[]{:S(2)}, u32[]{:S(2)}) async-start(f32[8,1,2048]{2,1,0:T(1,128)} %reshape.193), calls=%async_computation.15 | async-start | bytes 131072 | tf_op jit(solution)/shard_map/all_to_all | solution.py:134
  979.7 7.3 collective-permute-start.20
  (42 other events, 1767.8 us)
Sparse Core Ops, SparseCore 0:
  366.7 114.9 all-reduce.8
  702.6 76.8 all-reduce.10
